TPU v7x, 32 devices: a whole 2x2x4 slice. The times are simulated.
32 devices in a mesh: cls: 4 (over z), site: 8 (over y, x, core).
Axes of the slice: x: 2, y: 2, z: 4, core: 2. Of those that a mesh axis runs over, the one named last changes fastest.
Arguments:
- tip_codes: int32 [1024, 8192], P('cls', 'site'), may hold values from 0 to 3
- counts: int32 [8192], P('site'), may hold values from 1 to 5
- children: int32 [1023, 2], replicated, may hold values from 0 to 2045, as said below
- lengths: float32 [4, 2046], replicated, may hold values from 0.01 to 1
- frequencies: float32 [4, 4], replicated, may hold values from 0.25 to 1.75
- weights: float32 [4], replicated, may hold values from 0.2 to 1
Outputs:
- site_loglik: float32 [4, 2048], P('cls', 'site')
- new_weights: float32 [4], P('cls')
- mean_loglik: float32 [], replicated
Inputs may be any that keep to these rules, and one draw needn't show every extreme that they name: Row k lists the two children of internal node 1024 + k as node ids. Give the tips height 0 and the root height 10. The nodes of height h + 1 have exactly the nodes of height h as children, each once, and the root is node 2046. For every height h from 0 to 5, split the parents (height h + 1) and the children (height h) into 16 equal aligned blocks: the children of parent block j are child block j, so the tips j * 64 onward form clade j.
All inputs are finite; a program needn't handle non-finite values.
Results may differ from a plain program's by a relative error of at most 0.0003.
Values sent between devices are 32-bit elements; how exact they have to be, the bound alone decides.
A program may use at most 64 MiB of HBM per device.

v0:
```python
import jax
import jax.numpy as jnp
from jax import lax
from jax.sharding import PartitionSpec as P

LEVELS = 10
TOP = 4


def combined_all(array, axis, combine):
    everything = jax.tree.map(lambda part: lax.all_gather(part, axis), array)
    leading = jax.tree.map(lambda part: part[0], everything)

    def hop(k, so_far):
        return combine(so_far, jax.tree.map(lambda part: part[k], everything))

    return lax.fori_loop(1, lax.axis_size(axis), hop, leading)


def transit(values, decays, stationary):
    average = jnp.sum(stationary[:, None, None] * values, axis=0, keepdims=True)
    return decays[None, :, None] * values + (1.0 - decays)[None, :, None] * average


def join_pair(left_part, right_part, scale_sum):
    parent = left_part * right_part
    largest = jnp.max(parent, axis=0, keepdims=True)
    return (parent / largest, scale_sum + jnp.log(largest))


def rate_of(stationary):
    return 1.0 / (1.0 - jnp.sum(stationary * stationary))


def selector(child_ids, anchor, previous):
    both_rows = jnp.concatenate([child_ids[:, 0], child_ids[:, 1]]) - anchor
    columns = jnp.arange(previous, dtype=jnp.int32)
    return (both_rows[:, None] == columns[None, :]).astype(jnp.float32)


def pick_rows(select, source):
    return jnp.einsum("kn,ans->aks", select, source, precision=lax.Precision.HIGHEST)


def decays_of(child_ids, length_row, rate_scale):
    left_decay = jnp.exp(-rate_scale * jnp.take(length_row, child_ids[:, 0]))
    right_decay = jnp.exp(-rate_scale * jnp.take(length_row, child_ids[:, 1]))
    return (left_decay, right_decay)


def tip_level(code_floats, child_ids, anchor, length_row, stationary, rate_scale):
    node_count = child_ids.shape[0]
    select = selector(child_ids, anchor, code_floats.shape[0])
    picked = jnp.dot(select, code_floats, precision=lax.Precision.HIGHEST)
    states = jnp.arange(4, dtype=jnp.float32)
    onehot = (picked[None, :, :] == states[:, None, None]).astype(jnp.float32)
    left_decay, right_decay = decays_of(child_ids, length_row, rate_scale)
    left_part = transit(onehot[:, :node_count], left_decay, stationary)
    right_part = transit(onehot[:, node_count:], right_decay, stationary)
    scale_sum = jnp.zeros((1, node_count, code_floats.shape[1]), jnp.float32)
    return join_pair(left_part, right_part, scale_sum)


def level_up(values, scales, child_ids, anchor, length_row, stationary, rate_scale):
    node_count = child_ids.shape[0]
    select = selector(child_ids, anchor, values.shape[1])
    picked_values = pick_rows(select, values)
    picked_scales = pick_rows(select, scales)
    left_decay, right_decay = decays_of(child_ids, length_row, rate_scale)
    left_part = transit(picked_values[:, :node_count], left_decay, stationary)
    right_part = transit(picked_values[:, node_count:], right_decay, stationary)
    scale_sum = picked_scales[:, :node_count] + picked_scales[:, node_count:]
    return join_pair(left_part, right_part, scale_sum)


def lower_tree(code_floats, children, length_row, stationary, group_index, groups, taxa_count):
    rate_scale = rate_of(stationary)
    values = None
    scales = None
    for tree_level in range(LEVELS - TOP):
        node_count = (taxa_count >> tree_level + 1) // groups
        first_row = taxa_count - (taxa_count >> tree_level) + group_index * node_count
        child_ids = lax.dynamic_slice_in_dim(children, first_row, node_count, 0)
        if tree_level == 0:
            anchor = group_index * code_floats.shape[0]
            values, scales = tip_level(
                code_floats, child_ids, anchor, length_row, stationary, rate_scale
            )
        else:
            anchor = (
                taxa_count
                + taxa_count
                - (taxa_count >> tree_level - 1)
                + group_index * ((taxa_count >> tree_level) // groups)
            )
            values, scales = level_up(
                values, scales, child_ids, anchor, length_row, stationary, rate_scale
            )
    return (values, scales)


def upper_tree(values, scales, children, length_row, stationary, taxa_count):
    rate_scale = rate_of(stationary)
    for tree_level in range(LEVELS - TOP, LEVELS):
        node_count = taxa_count >> tree_level + 1
        offset = taxa_count - (taxa_count >> tree_level)
        child_ids = children[offset : offset + node_count]
        anchor = taxa_count + taxa_count - (taxa_count >> tree_level - 1)
        values, scales = level_up(
            values, scales, child_ids, anchor, length_row, stationary, rate_scale
        )
    return scales[0, 0] + jnp.log(jnp.sum(stationary[:, None] * values[:, 0], axis=0))


def combine_parts(earlier, later_one):
    largest = jnp.maximum(earlier[0], later_one[0])
    mass = earlier[1] * jnp.exp(earlier[0] - largest) + later_one[1] * jnp.exp(
        later_one[0] - largest
    )
    return (largest, mass)


def per_device(tip_codes, counts, children, lengths, frequencies, weights):
    groups = lax.axis_size("cls")
    group_index = lax.axis_index("cls")
    taxa_count = tip_codes.shape[0] * groups
    site_count = tip_codes.shape[1]
    quarter = site_count // groups
    classes = lengths.shape[0]
    stationary = frequencies / jnp.sum(frequencies, axis=1, keepdims=True)
    log_weight = jnp.log(weights / jnp.sum(weights))
    code_floats = tip_codes.astype(jnp.float32)
    low_values = []
    low_scales = []
    for class_no in range(classes):
        part_values, part_scales = lower_tree(
            code_floats,
            children,
            lengths[class_no],
            stationary[class_no],
            group_index,
            groups,
            taxa_count,
        )
        low_values.append(part_values)
        low_scales.append(part_scales)
    stacked_values = jnp.stack(low_values)
    stacked_scales = jnp.stack(low_scales)
    pattern_weight = counts.astype(jnp.float32)
    clade_values, clade_scales = (
        lax.all_to_all(stacked_values, "cls", split_axis=0, concat_axis=2, tiled=True),
        lax.all_to_all(stacked_scales, "cls", split_axis=0, concat_axis=2, tiled=True),
    )
    own_lengths = lax.dynamic_index_in_dim(lengths, group_index, 0, keepdims=False)
    own_stationary = lax.dynamic_index_in_dim(stationary, group_index, 0, keepdims=False)
    class_ll = upper_tree(
        clade_values[0], clade_scales[0], children, own_lengths, own_stationary, taxa_count
    )
    shifted = class_ll + lax.dynamic_index_in_dim(log_weight, group_index, 0, keepdims=False)
    largest, mass = combined_all((shifted, jnp.ones_like(shifted)), "cls", combine_parts)
    site_total = largest + jnp.log(mass)
    posterior = jnp.exp(shifted - site_total)
    sum_loglik, class_mass, all_count = lax.psum(
        (
            jnp.sum(pattern_weight * site_total),
            jnp.sum(pattern_weight * posterior),
            jnp.sum(pattern_weight),
        ),
        "site",
    )
    new_weights = (class_mass / all_count).reshape(1)
    own_sites = lax.dynamic_slice_in_dim(site_total, group_index * quarter, quarter, 0)
    per_taxon = (own_sites / taxa_count).reshape(1, quarter)
    mean_loglik = sum_loglik / (all_count * taxa_count)
    return (per_taxon, new_weights, mean_loglik)


def solution(mesh):
    return jax.shard_map(
        per_device,
        mesh=mesh,
        in_specs=(P("cls", "site"), P("site"), P(), P(), P(), P()),
        out_specs=(P("cls", "site"), P("cls"), P()),
        check_vma=False,
    )
```

profile of v0, /device:TPU:0, one launch (start us, length us, event | category | flops | bytes accessed | tf_op | source)
XLA Modules:
  0.0 151.5 jit_solution(7130385078546404520)
XLA Ops:
  0.7 0.8 constant_dynamic-slice_fusion.7
  1.5 0.8 constant_dynamic-slice_fusion.8
  2.3 1.0 constant_dynamic-slice_fusion.1
  3.3 1.1 gather_fusion
  4.5 1.1 gather_fusion.1
  5.6 1.1 gather_fusion.24
  6.8 1.1 gather_fusion.25
  7.9 1.1 gather_fusion.36
  9.1 1.1 gather_fusion.37
  10.5 0.7 multiply_reduce_fusion.58
  11.2 1.1 gather_fusion.13
  12.5 0.8 gather_fusion.3
  13.3 0.8 gather_fusion.15
  14.1 0.8 gather_fusion.2
  14.8 0.8 gather_fusion.26
  15.6 0.8 gather_fusion.27
  16.4 0.8 gather_fusion.38
  17.2 0.8 gather_fusion.39
  18.1 0.7 gather_fusion.5
  18.8 0.7 gather_fusion.17
  19.5 0.7 gather_fusion.4
  20.2 0.7 gather_fusion.28
  20.9 0.7 gather_fusion.29
  21.6 0.7 gather_fusion.40
  22.3 0.7 gather_fusion.41
  23.2 0.7 gather_fusion.7
  23.8 0.7 gather_fusion.19
  24.5 0.7 gather_fusion.6
  25.1 0.7 gather_fusion.30
  25.8 0.7 gather_fusion.31
  26.5 0.7 gather_fusion.42
  27.1 0.7 gather_fusion.43
  28.5 0.6 gather_fusion.21
  29.8 0.6 gather_fusion.32
  30.4 0.6 gather_fusion.33
  31.1 0.6 gather_fusion.44
  37.0 1.1 gather_fusion.12
  38.1 0.8 gather_fusion.14
  38.9 0.7 gather_fusion.16
  39.6 0.7 gather_fusion.18
  44.3 0.7 fusion.30
  45.6 1.4 multiply_reduce_fusion.7
  47.7 3.6 %fusion.348 = (f32[128,1024]{1,0:T(8,128)S(1)}, f32[4,128,1024]{2,1,0:T(8,128)S(1)}, f32[128,1024]{1,0:T(8,128)S(1)}, f32[4,128,1024]{2,1,0:T(8,128)}, f32[128,1024]{1,0:T(8,128)S(1)}, /*index=5*/f32[4,128,1024]{2,1,0:T(8,128)}) fusion(f32[128,1024]{1,0:T(8,128)S(1)} %broadcast_multiply_fusion.6, f32[4,256,1024]{2,1,0:T(8,128)S(1)} %fusion.1, ...), kind=kLoop, calls=%fused_computation.785 | loop fusion | flops 9043968 | bytes 15207424 | tf_op jit(solution)/shard_map/reduce_max | solution.py:27
  51.8 1.6 %fusion.10 = f32[4,128,1024]{2,1,0:T(8,128)S(1)} fusion(f32[4,128,1024]{2,1,0:T(8,128)S(1)} %get-tuple-element.309, f32[128,1024]{1,0:T(8,128)S(1)} %get-tuple-element.308, s32[128]{0:T(128)S(1)} %get-tuple-element.565), kind=kOutput, calls=%fused_computation.79 | convolution fusion | flops 805847040 | bytes 4719104 | tf_op jit(solution)/shard_map/kn,ans->aks/dot_general | solution.py:42
  54.7 0.7 convolution_bitcast_fusion.3
  59.0 3.0 %fusion.366 = (f32[128,1024]{1,0:T(8,128)S(1)}, f32[4,128,1024]{2,1,0:T(8,128)S(1)}) fusion(f32[128,1024]{1,0:T(8,128)S(1)} %broadcast_multiply_fusion.4, f32[4,256,1024]{2,1,0:T(8,128)} %copy-done, f32[128]{0:T(128)S(1)} %get-tuple-element.528, f32[128,1024]{1,0:T(8,128)S(1)} %broadcast_multiply_fusion.5, f32[128]{0:T(128)S(1)} %get-tuple-element.347), kind=kLoop, calls=%fused_computation.791 | loop fusion | flops 3014656 | bytes 7865344 | tf_op jit(solution)/shard_map/reduce_max | solution.py:27
  62.5 1.6 %fusion.13 = f32[4,128,1024]{2,1,0:T(8,128)S(1)} fusion(f32[4,128,1024]{2,1,0:T(8,128)S(1)} %get-tuple-element.345, f32[128,1024]{1,0:T(8,128)S(1)} %get-tuple-element.344, s32[128]{0:T(128)S(1)} %get-tuple-element.565), kind=kOutput, calls=%fused_computation.80 | convolution fusion | flops 805847040 | bytes 4719104 | tf_op jit(solution)/shard_map/kn,ans->aks/dot_general | solution.py:42
  65.4 0.7 convolution_bitcast_fusion.2
  69.8 1.8 %fusion.16 = f32[4,128,1024]{2,1,0:T(8,128)S(1)} fusion(f32[4,128,1024]{2,1,0:T(8,128)S(1)} %copy-done.2, f32[128,1024]{1,0:T(8,128)S(1)} %get-tuple-element.422, s32[128]{0:T(128)S(1)} %get-tuple-element.565), kind=kOutput, calls=%fused_computation.81 | convolution fusion | flops 805847040 | bytes 4719104 | tf_op jit(solution)/shard_map/kn,ans->aks/dot_general | solution.py:42
  72.9 0.7 convolution_bitcast_fusion.1
  77.3 1.6 %fusion.19 = f32[4,128,1024]{2,1,0:T(8,128)S(1)} fusion(f32[4,128,1024]{2,1,0:T(8,128)S(1)} %copy-done.1, f32[128,1024]{1,0:T(8,128)S(1)} %get-tuple-element.424, s32[128]{0:T(128)S(1)} %get-tuple-element.565), kind=kOutput, calls=%fused_computation.82 | convolution fusion | flops 805847040 | bytes 4719104 | tf_op jit(solution)/shard_map/kn,ans->aks/dot_general | solution.py:42
  80.2 0.7 convolution_bitcast_fusion
  85.8 6.3 %all-to-all-start = ((f32[4,1,4,1024]{3,2,1,0:T(4,128)}), f32[4,1,4,1024]{3,2,1,0:T(4,128)S(1)}, u32[]{:S(2)}, u32[]{:S(2)}) async-start(f32[4,1,4,1024]{3,2,1,0:T(4,128)} %pad_maximum_fusion.1), calls=%async_computation | async-start | bytes 131072 | tf_op jit(solution)/shard_map/all_to_all | solution.py:152
  92.4 0.7 fusion.406
  96.4 1.4 compare_select_fusion.1
  98.5 0.7 divide_log_fusion
  99.4 0.8 pad_maximum_fusion
  100.2 5.1 %all-to-all-start.1 = ((f32[4,4,4,1024]{3,2,1,0:T(4,128)}), f32[4,4,4,1024]{3,2,1,0:T(4,128)S(1)}, u32[]{:S(2)}, u32[]{:S(2)}) async-start(f32[4,4,4,1024]{3,2,1,0:T(4,128)} %pad_maximum_fusion), calls=%async_computation.1 | async-start | bytes 524288 | tf_op jit(solution)/shard_map/all_to_all | solution.py:151
  110.7 1.4 fusion.405
  117.7 0.7 fusion.243
  118.4 13.8 %all-gather = f32[4,1,1024]{2,1,0:T(1,128)S(1)} all-gather(f32[1,1,1024]{2,1,0:T(1,128)S(1)} %get-tuple-element.254), channel_id=1, replica_groups=mesh['cls'=4,'site'=8] {'cls'}, dimensions={0}, use_global_device_ids=true | all-gather | bytes 20480 | tf_op jit(solution)/shard_map/all_gather | solution.py:11
  132.3 1.3 multiply_reduce_fusion.56
  133.7 12.5 %all-reduce = (f32[]{:T(128)}, f32[]{:T(128)}, f32[]{:T(128)}) all-reduce(f32[]{:T(128)} %get-tuple-element.234, f32[]{:T(128)} %get-tuple-element.235, f32[]{:T(128)} %get-tuple-element.233), channel_id=1, replica_groups=mesh['cls'=4,'site'=8] {'site'}, use_global_device_ids=true, to_apply=%region_95.103 | all-reduce | flops 3 | bytes 24 | tf_op jit(solution)/shard_map/psum | solution.py:163
  148.6 0.6 dynamic-slice_multiply_fusion
  (268 shorter events, 40.8 us)
Async XLA Ops:
  0.6 11.7 %copy-start.4 = (s32[1023,2]{0,1:T(2,128)S(1)}, s32[1023,2]{0,1:T(2,128)}, u32[]{:S(2)}) copy-start(s32[1023,2]{0,1:T(2,128)} %param.24) | copy-start | bytes 24556
  0.6 9.6 %copy-start.5 = (f32[4,4]{1,0:T(4,128)S(1)}, f32[4,4]{1,0:T(4,128)}, u32[]{:S(2)}) copy-start(f32[4,4]{1,0:T(4,128)} %param.26) | copy-start | bytes 196
  35.7 8.6 %copy-start.3 = (s32[256,1024]{1,0:T(8,128)S(1)}, s32[256,1024]{1,0:T(8,128)}, u32[]{:S(2)}) copy-start(s32[256,1024]{1,0:T(8,128)} %param.22) | copy-start | bytes 3145732
  45.6 2.1 %copy-start = (f32[4,256,1024]{2,1,0:T(8,128)}, f32[4,256,1024]{2,1,0:T(8,128)S(1)}, u32[]{:S(2)}) copy-start(f32[4,256,1024]{2,1,0:T(8,128)S(1)} %fusion.1) | copy-start | bytes 12582916
  67.8 2.0 %copy-start.2 = (f32[4,128,1024]{2,1,0:T(8,128)S(1)}, f32[4,128,1024]{2,1,0:T(8,128)}, u32[]{:S(2)}) copy-start(f32[4,128,1024]{2,1,0:T(8,128)} %get-tuple-element.423) | copy-start | bytes 6291460
  75.3 2.0 %copy-start.1 = (f32[4,128,1024]{2,1,0:T(8,128)S(1)}, f32[4,128,1024]{2,1,0:T(8,128)}, u32[]{:S(2)}) copy-start(f32[4,128,1024]{2,1,0:T(8,128)} %get-tuple-element.425) | copy-start | bytes 6291460
  84.3 13.6 %copy-start.7 = (f32[4]{0:T(128)S(1)}, f32[4]{0:T(128)}, u32[]{:S(2)}) copy-start(f32[4]{0:T(128)} %param.27) | copy-start | bytes 52
  85.8 14.4 %all-to-all-start = ((f32[4,1,4,1024]{3,2,1,0:T(4,128)}), f32[4,1,4,1024]{3,2,1,0:T(4,128)S(1)}, u32[]{:S(2)}, u32[]{:S(2)}) async-start(f32[4,1,4,1024]{3,2,1,0:T(4,128)} %pad_maximum_fusion.1), calls=%async_computation | async-start | bytes 131072 | tf_op jit(solution)/shard_map/all_to_all | solution.py:152
  100.2 14.0 %all-to-all-start.1 = ((f32[4,4,4,1024]{3,2,1,0:T(4,128)}), f32[4,4,4,1024]{3,2,1,0:T(4,128)S(1)}, u32[]{:S(2)}, u32[]{:S(2)}) async-start(f32[4,4,4,1024]{3,2,1,0:T(4,128)} %pad_maximum_fusion), calls=%async_computation.1 | async-start | bytes 524288 | tf_op jit(solution)/shard_map/all_to_all | solution.py:151
  114.9 17.5 %copy-start.6 = (s32[1024]{0:T(1024)S(1)}, s32[1024]{0:T(1024)}, u32[]{:S(2)}) copy-start(s32[1024]{0:T(1024)} %param.23) | copy-start | bytes 12292
where the time goes:
time: 152 us
  local copies, waits for them, and re-layouts  46.2 us (30%)
  other arithmetic  30 us (20%)
  blocking collectives  26.3 us (17%)
  matrix products  22.2 us (15%)
  between operations  15.3 us (10%)
  starting transfers between devices  11.4 us (8%)
    gather x28, local copies, waits for them, and re-layouts, decays_of(): left_decay = jnp.exp(-rate_scale * jnp.take(length_row, child_ids[:, 0]))  21.5 us
    dot_general x48, matrix products, pick_rows(): jnp.einsum('kn,ans->aks', select, source, precision=lax.Precision.HIGHEST)  21.4 us
    gather x27, local copies, waits for them, and re-layouts, decays_of(): right_decay = jnp.exp(-rate_scale * jnp.take(length_row, child_ids[:, 1]))  20.1 us
    all_gather x1, blocking collectives, combined_all(): everything = jax.tree.map(lambda part: lax.all_gather(part, axis), array)  13.8 us
    psum x1, blocking collectives, per_device(): lax.psum((jnp.sum(pattern_weight * site_total), jnp.sum(pattern_weight *...  12.5 us
    reduce_max x26, other arithmetic, join_pair(): largest = jnp.max(parent, axis=0, keepdims=True)  11.1 us
    all_to_all x1, starting transfers between devices, per_device(): lax.all_to_all(stacked_scales, 'cls', split_axis=0, concat_axis=2, tiled=...  6.35 us
    all_to_all x1, starting transfers between devices, per_device(): lax.all_to_all(stacked_values, 'cls', split_axis=0, concat_axis=2, tiled=...  5.09 us
  transfers between devices with their start and end apart: 2, of which 0 were waited for; matrix products, arithmetic and copies ran while one was open for 7% of the time, Pallas kernels for 0%

commit v1 on v0

v1 whole, which is shorter than its diff:
```python
import functools

import jax
import jax.numpy as jnp
from jax import lax
from jax.experimental import pallas as pl
from jax.experimental.pallas import tpu as pltpu
from jax.sharding import PartitionSpec as P

LEVELS = 10
TOP = 4
LANES = 128
MESH = pl.DeviceIdType.MESH


def level_base(taxa, h):
    return 0 if h == 0 else 2 * taxa - (taxa >> (h - 1))


def kernel(
    groups,
    site_devices,
    codes_hbm,
    counts_ref,
    kids_ref,
    kids_smem,
    lengths_ref,
    freq_ref,
    weights_ref,
    site_out,
    weight_out,
    mean_out,
    codes,
    picked,
    table,
    grow,
    grow_up,
    stat,
    sent,
    got,
    upper,
    part,
    part_got,
    group_sum,
    group_got,
    code_sem,
    send_sem,
    recv_sem,
    part_send,
    part_recv,
    sum_send,
    sum_recv,
):
    g = lax.axis_index("cls")
    me = lax.axis_index("site")
    local, sites = codes_hbm.shape
    taxa = local * groups
    classes, branches = lengths_ref.shape
    quarter = sites // groups
    halves = quarter // LANES
    low = LEVELS - TOP
    clades = local >> low
    rows = halves * classes
    f32 = jnp.float32
    bf16 = jnp.bfloat16

    fetch = pltpu.make_async_copy(codes_hbm, codes, code_sem)
    fetch.start()

    barrier = pltpu.get_barrier_semaphore()
    for k in range(1, groups):
        pl.semaphore_signal(
            barrier, inc=1, device_id={"cls": lax.rem(g + k, groups)}, device_id_type=MESH
        )
    for k in range(1, site_devices):
        pl.semaphore_signal(
            barrier,
            inc=1,
            device_id={"site": lax.rem(me + k, site_devices)},
            device_id_type=MESH,
        )

    freq = freq_ref[...]
    pi = freq / jnp.sum(freq, axis=1, keepdims=True)
    beta = 1.0 / (1.0 - jnp.sum(pi * pi, axis=1, keepdims=True))
    lengths = lengths_ref[...]
    r = jnp.exp(beta * lengths) - 1.0
    drift = beta * jnp.sum(lengths, axis=1, keepdims=True)

    table[...] = jnp.zeros_like(table)
    hi = r.astype(bf16).astype(f32)
    rest = r - hi
    mid = rest.astype(bf16).astype(f32)
    table[0:classes, 0:branches] = hi
    table[classes : 2 * classes, 0:branches] = mid
    table[2 * classes : 3 * classes, 0:branches] = rest - mid
    kids = kids_ref[...]
    table[12:14, taxa : taxa + kids.shape[1]] = (kids >> 8).astype(f32)
    table[14:16, taxa : taxa + kids.shape[1]] = (kids & 255).astype(f32)

    pi8 = jnp.concatenate([pi] * halves, axis=0)
    for c in range(classes):
        for i in range(4):
            wide = jnp.broadcast_to(pi[:, i : i + 1], (classes, LANES))
            stat[c, i] = jnp.broadcast_to(wide[c : c + 1], (8, LANES))
    first_up = level_base(taxa, low)
    window = first_up // LANES * LANES
    r8 = jnp.concatenate([r[:, window:branches]] * halves, axis=0)
    for j in range(branches - first_up):
        at = first_up - window + j
        grow_up[j] = jnp.broadcast_to(r8[:, at : at + 1], (rows, LANES))

    q = lax.broadcasted_iota(jnp.int32, (1, local), 1)
    ancestor = (first_up + g * clades + (q & (clades - 1))).astype(f32)
    offset = {}
    total_rows = 0
    for h in range(low):
        offset[h] = total_rows
        total_rows += local >> h
    for h in range(low, -1, -1):
        count = local >> h
        base = level_base(taxa, h)
        if count % LANES == 0:
            start = pl.multiple_of(base + g * count, LANES)
            width = count
        else:
            start = base // LANES * LANES
            end = base + (taxa >> h)
            width = -(-end // LANES) * LANES - start
        ids = lax.broadcasted_iota(jnp.int32, (width, local), 0) + start
        onehot = (ids.astype(f32) == ancestor).astype(f32).astype(bf16)
        part_table = table[:, pl.ds(start, width)].astype(bf16)
        out = jnp.dot(part_table, onehot, preferred_element_type=f32)
        if h < low:
            r_row = out[0:classes] + out[classes : 2 * classes] + out[2 * classes : 3 * classes]
            r_col = jnp.concatenate([r_row, r_row], axis=0).T
            for c in range(classes):
                grow[c, offset[h] : offset[h] + count, :] = jnp.broadcast_to(
                    r_col[:count, c : c + 1], (count, LANES)
                )
        if h > 0:
            left = out[12:13] * 256.0 + out[14:15]
            right = out[13:14] * 256.0 + out[15:16]
            ancestor = jnp.where((q & count) != 0, right, left)
    tip_col = jnp.broadcast_to(ancestor, (8, local)).T[:, 0:1]
    tip_ids = (lax.broadcasted_iota(jnp.int32, (local, local), 1) + g * local).astype(f32)
    order = (tip_ids == tip_col).astype(f32).astype(bf16)

    fetch.wait()

    def quarter_of(k, dest):
        block = lax.rem(g + k, groups)
        for half in range(halves):
            lanes = pl.ds(pl.multiple_of(block * quarter + half * LANES, LANES), LANES)
            picked[half] = jnp.dot(
                order, codes[:, lanes].astype(f32).astype(bf16), preferred_element_type=f32
            )

        def one(step, carry):
            half = step // classes
            c = lax.rem(step, classes)
            pis = [stat[c, i] for i in range(4)]

            def factor(h, n):
                return grow[c, offset[h] + 8 * n : offset[h] + 8 * n + 8, :]

            def tip(n):
                code = picked[half, 8 * n : 8 * n + 8, :]
                marks = [code == float(i) for i in range(4)]
                own = jnp.where(
                    marks[0], pis[0], jnp.where(marks[1], pis[1], jnp.where(marks[2], pis[2], pis[3]))
                )
                off = factor(0, n) * own
                on = off + 1.0
                return [jnp.where(mark, on, off) for mark in marks]

            def spread(values, scale):
                mean = (values[0] * pis[0] + values[1] * pis[1]) + (
                    values[2] * pis[2] + values[3] * pis[3]
                )
                move = scale * mean
                return [value + move for value in values]

            logs = []

            def node(h, n):
                if h == 0:
                    return tip(n)
                gap = (local >> h) // 8
                left = node(h - 1, n)
                right = node(h - 1, n + gap)
                if h > 1:
                    left = spread(left, factor(h - 1, n))
                    right = spread(right, factor(h - 1, n + gap))
                values = [a * b for a, b in zip(left, right)]
                if h == 3:
                    largest = jnp.maximum(
                        jnp.maximum(values[0], values[1]), jnp.maximum(values[2], values[3])
                    )
                    scale = pl.reciprocal(largest, approx=True)
                    logs.append(jnp.log(scale))
                    values = [value * scale for value in values]
                return values

            values = spread(node(low - 1, 0), factor(low - 1, 0))
            values = [value[0:clades] * value[clades : 2 * clades] for value in values]
            log_sum = jnp.sum(sum(logs[1:], logs[0]), axis=0, keepdims=True)
            log_sum = jnp.sum(jnp.log(values[3]), axis=0, keepdims=True) - log_sum
            inverse = 1.0 / values[3]
            for i in range(3):
                ratio = values[i] * inverse
                for j in range(clades):
                    dest[j * 3 + i, pl.ds(step, 1), :] = ratio[j : j + 1]
            dest[clades * 3, pl.ds(step, 1), :] = log_sum
            return carry

        lax.fori_loop(0, rows, one, 0)

    copies = []
    for place, k in enumerate([2, 1, 3] if groups == 4 else range(1, groups)):
        quarter_of(k, sent.at[k])
        if place == 0:
            pl.semaphore_wait(barrier, groups + site_devices - 2)
        copy = pltpu.make_async_remote_copy(
            src_ref=sent.at[k],
            dst_ref=got.at[k],
            send_sem=send_sem.at[k],
            recv_sem=recv_sem.at[k],
            device_id={"cls": lax.rem(g + k, groups)},
            device_id_type=MESH,
        )
        copy.start()
        copies.append(copy)
    quarter_of(0, got.at[0])
    for copy in copies:
        copy.wait()

    pis8 = [jnp.broadcast_to(pi8[:, i : i + 1], (rows, LANES)) for i in range(4)]
    scales = got[0, clades * 3]
    for k in range(1, groups):
        scales = scales + got[k, clades * 3]

    def child(tree_level, ident):
        if tree_level == low:
            clade = jnp.clip(ident - first_up, 0, 2**TOP - 1)
            k = lax.rem(g + groups - clade // clades, groups)
            row = lax.rem(clade, clades) * 3
            values = [got[k, row + i] for i in range(3)] + [jnp.ones((rows, LANES), f32)]
        else:
            at = jnp.clip(ident - level_base(taxa, low + 1), 0, 2**TOP - 1)
            values = [upper[at, i] for i in range(4)]
        mean = (values[0] * pis8[0] + values[1] * pis8[1]) + (
            values[2] * pis8[2] + values[3] * pis8[3]
        )
        move = grow_up[jnp.clip(ident - first_up, 0, branches - first_up - 1)] * mean
        return [value + move for value in values]

    place = 0
    for tree_level in range(low, LEVELS):
        count = taxa >> (tree_level + 1)
        first = taxa - (taxa >> tree_level)
        for n in range(count):
            left = child(tree_level, kids_smem[0, first + n])
            right = child(tree_level, kids_smem[1, first + n])
            values = [a * b for a, b in zip(left, right)]
            largest = jnp.maximum(
                jnp.maximum(values[0], values[1]), jnp.maximum(values[2], values[3])
            )
            scale = pl.reciprocal(largest, approx=True)
            scales = scales - jnp.log(scale)
            values = [value * scale for value in values]
            if tree_level < LEVELS - 1:
                for i in range(4):
                    upper[place, i] = values[i]
                place += 1
    end = (values[0] * pis8[0] + values[1] * pis8[1]) + (
        values[2] * pis8[2] + values[3] * pis8[3]
    )
    spot = lax.broadcasted_iota(jnp.int32, (classes, classes), 0)
    spot = spot == lax.broadcasted_iota(jnp.int32, (classes, classes), 1)
    weights = jnp.sum(jnp.where(spot, weights_ref[...], 0.0), axis=1, keepdims=True)
    log_weight = jnp.log(weights / jnp.sum(weights, axis=0, keepdims=True))
    bias = jnp.concatenate([log_weight - drift] * halves, axis=0)
    shifted = scales + jnp.log(end) + bias

    mass = jnp.zeros((classes, LANES), f32)
    loglik = jnp.zeros((1, LANES), f32)
    seen = jnp.zeros((1, LANES), f32)
    for half in range(halves):
        a = shifted[half * classes : (half + 1) * classes]
        top = jnp.max(a, axis=0, keepdims=True)
        total = top + jnp.log(jnp.sum(jnp.exp(a - top), axis=0, keepdims=True))
        n = counts_ref[pl.ds(g * halves + half, 1), :].astype(f32)
        site_out[0:1, half * LANES : (half + 1) * LANES] = total / taxa
        mass = mass + n * jnp.exp(a - total)
        loglik = loglik + n * total
        seen = seen + n
    part[...] = jnp.zeros_like(part)
    part[0:classes] = mass
    part[classes : classes + 1] = loglik
    part[classes + 1 : classes + 2] = seen

    copies = []
    for k in range(1, groups):
        copy = pltpu.make_async_remote_copy(
            src_ref=part,
            dst_ref=part_got.at[k],
            send_sem=part_send.at[k],
            recv_sem=part_recv.at[k],
            device_id={"cls": lax.rem(g + k, groups)},
            device_id_type=MESH,
        )
        copy.start()
        copies.append(copy)
    for copy in copies:
        copy.wait()
    part_got[0] = part[...]
    sums = part_got[lax.rem(g + groups, groups)]
    for d in range(1, groups):
        sums = sums + part_got[lax.rem(g + groups - d, groups)]
    group_sum[...] = sums
    copies = []
    for k in range(1, site_devices):
        copy = pltpu.make_async_remote_copy(
            src_ref=group_sum,
            dst_ref=group_got.at[k],
            send_sem=sum_send.at[k],
            recv_sem=sum_recv.at[k],
            device_id={"site": lax.rem(me + k, site_devices)},
            device_id_type=MESH,
        )
        copy.start()
        copies.append(copy)
    for copy in copies:
        copy.wait()
    group_got[0] = sums
    sums = group_got[lax.rem(me + site_devices, site_devices)]
    for d in range(1, site_devices):
        sums = sums + group_got[lax.rem(me + site_devices - d, site_devices)]
    line = jnp.sum(sums, axis=1, keepdims=True)
    all_count = line[classes + 1 : classes + 2]
    mean = line[classes : classes + 1] / (all_count * taxa)
    share = line[0:classes] / all_count
    mine = lax.broadcasted_iota(jnp.int32, (classes, 1), 0) == g
    weight_out[0] = jnp.sum(jnp.where(mine, share, 0.0))
    mean_out[0] = jnp.sum(mean)


def solution(mesh):
    groups = mesh.shape["cls"]
    site_devices = mesh.shape["site"]

    def per_device(tip_codes, counts, children, lengths, frequencies, weights):
        local, sites = tip_codes.shape
        taxa = local * groups
        classes, branches = lengths.shape
        quarter = sites // groups
        halves = quarter // LANES
        rows = halves * classes
        low = LEVELS - TOP
        clades = local >> low
        low_rows = sum(local >> h for h in range(low))
        table_width = -(-(branches + 1) // LANES) * LANES
        up_count = branches - level_base(taxa, low)
        kids = children.T
        vmem = pl.BlockSpec(memory_space=pltpu.VMEM)
        smem = pl.BlockSpec(memory_space=pltpu.SMEM)
        f32 = jnp.float32
        site_loglik, new_weights, mean_loglik = pl.pallas_call(
            functools.partial(kernel, groups, site_devices),
            out_shape=(
                jax.ShapeDtypeStruct((1, quarter), f32),
                jax.ShapeDtypeStruct((1,), f32),
                jax.ShapeDtypeStruct((1,), f32),
            ),
            in_specs=[pl.BlockSpec(memory_space=pl.ANY), vmem, vmem, smem, vmem, vmem, vmem],
            out_specs=(vmem, smem, smem),
            scratch_shapes=[
                pltpu.VMEM((local, sites), jnp.int32),
                pltpu.VMEM((halves, local, LANES), f32),
                pltpu.VMEM((16, table_width), f32),
                pltpu.VMEM((classes, low_rows, LANES), f32),
                pltpu.VMEM((up_count, rows, LANES), f32),
                pltpu.VMEM((classes, 4, 8, LANES), f32),
                pltpu.VMEM((groups, clades * 3 + 1, rows, LANES), f32),
                pltpu.VMEM((groups, clades * 3 + 1, rows, LANES), f32),
                pltpu.VMEM((2 ** TOP, 4, rows, LANES), f32),
                pltpu.VMEM((8, LANES), f32),
                pltpu.VMEM((groups, 8, LANES), f32),
                pltpu.VMEM((8, LANES), f32),
                pltpu.VMEM((site_devices, 8, LANES), f32),
                pltpu.SemaphoreType.DMA,
                pltpu.SemaphoreType.DMA((groups,)),
                pltpu.SemaphoreType.DMA((groups,)),
                pltpu.SemaphoreType.DMA((groups,)),
                pltpu.SemaphoreType.DMA((groups,)),
                pltpu.SemaphoreType.DMA((site_devices,)),
                pltpu.SemaphoreType.DMA((site_devices,)),
            ],
            compiler_params=pltpu.CompilerParams(collective_id=0, has_side_effects=True),
        )(
            tip_codes,
            counts.reshape(sites // LANES, LANES),
            kids,
            kids,
            lengths,
            frequencies,
            weights.reshape(1, classes),
        )
        return site_loglik, new_weights, mean_loglik.reshape(())

    return jax.shard_map(
        per_device,
        mesh=mesh,
        in_specs=(P("cls", "site"), P("site"), P(), P(), P(), P()),
        out_specs=(P("cls", "site"), P("cls"), P()),
        check_vma=False,
    )
```

time: 152 us -> 27.9 us (0.18)
  local copies, waits for them, and re-layouts: 46.2 us -> 1.21 us
  other arithmetic: 30 us -> 0 us
  blocking collectives: 26.3 us -> 0 us
  Pallas kernels: 0 us -> 22.3 us
  matrix products: 22.2 us -> 0 us
  starting transfers between devices: 11.4 us -> 0 us
  between operations: 15.3 us -> 4.14 us
    gather x55 -> x0, local copies, waits for them, and re-layouts: 41.6 us -> none  [the longest x28 21.5 us: decays_of(): left_decay = jnp.exp(-rate_scale * jnp.take(length_row, child_ids[:, 0]))]
    pallas_call x0 -> x1, Pallas kernels: none -> 22.3 us  [per_device(): pl.pallas_call(functools.partial(kernel, groups, site_devices), out_shape...]
    dot_general x49 -> x0, matrix products: 22.2 us -> none  [the longest x48 21.4 us: pick_rows(): jnp.einsum('kn,ans->aks', select, source, precision=lax.Precision.HIGHEST)]
    all_gather x1 -> x0, blocking collectives: 13.8 us -> none  [combined_all(): everything = jax.tree.map(lambda part: lax.all_gather(part, axis), array)]
    psum x1 -> x0, blocking collectives: 12.5 us -> none  [per_device(): lax.psum((jnp.sum(pattern_weight * site_total), jnp.sum(pattern_weight *...]
    all_to_all x2 -> x0, starting transfers between devices: 11.4 us -> none  [the longest x1 6.35 us: per_device(): lax.all_to_all(stacked_scales, 'cls', split_axis=0, concat_axis=2, tiled=...]
    reduce_max x26 -> x0, other arithmetic: 11.1 us -> none  [join_pair(): largest = jnp.max(parent, axis=0, keepdims=True)]
    reduce_sum x30 -> x0, other arithmetic: 7.67 us -> none  [the longest x25 4.81 us: transit(): average = jnp.sum(stationary[:, None, None] * values, axis=0, keepdims=True)]
  transfers between devices with their start and end apart: 2 -> 0, of which waited for: 0 -> 0; matrix products, arithmetic and copies ran while one was open for 7% -> 0% of each run, Pallas kernels for 0% -> 0%
where the time goes in v1:
time: 27.9 us; the launch traced here: 27.6 us
  Pallas kernels  22.3 us (80%)
  between operations  4.14 us (15%)
  local copies, waits for them, and re-layouts  1.21 us (4%)
    pallas_call x1, Pallas kernels, per_device(): pl.pallas_call(functools.partial(kernel, groups, site_devices), out_shape...  22.3 us
    unnamed x3, local copies, waits for them, and re-layouts  1.21 us

profile of v1, /device:TPU:0, one launch (start us, length us, event | category | flops | bytes accessed | tf_op | source)
XLA Modules:
  0.0 27.6 jit_solution(12306021058523377330)
XLA Ops:
  0.6 22.3 %shard_map.85 = (f32[1,256]{1,0:T(1,128)}, f32[1]{0:T(128)}, f32[1]{0:T(128)}) custom-call(s32[256,1024]{1,0:T(8,128)} %codes_hbm.1, s32[8,128]{1,0:T(8,128)} %bitcast.6, s32[2,1023]{1,0:T(2,128)} %bitcast.4, s32[2,1023]{1,0:T(2,128)} %bitcast.5, f32[4,2046]{1,0:T(4,128)} %lengths_ref.1, f32[4,4]{1,0:T(4,128)} %freq_ref.1, f32[1,4]{1,0:T(1,128)} %bitcast.7), custom_call_target="tpu_custom_call" | custom-call | tf_op jit(solution)/shard_map/pallas_call | solution.py:369
  22.9 0.0 copy-start
  22.9 0.6 %copy-done = f32[1,256]{1,0:T(1,128)S(1)} copy-done((f32[1,256]{1,0:T(1,128)S(1)}, f32[1,256]{1,0:T(1,128)}, u32[]{:S(2)}) %copy-start) | copy-done | bytes 1048
  23.6 0.6 %copy.12 = f32[1,256]{1,0:T(1,128)} copy(f32[1,256]{1,0:T(1,128)S(1)} %copy-done) | data formatting | bytes 2048
Async XLA Ops:
  22.9 0.7 %copy-start = (f32[1,256]{1,0:T(1,128)S(1)}, f32[1,256]{1,0:T(1,128)}, u32[]{:S(2)}) copy-start(f32[1,256]{1,0:T(1,128)} %get-tuple-element.12) | copy-start | bytes 3076

commit v2 on v1

--- a/solution.py
+++ b/solution.py
@@ -27,9 +27,7 @@
     lengths_ref,
     freq_ref,
     weights_ref,
-    site_out,
-    weight_out,
-    mean_out,
+    result,
     codes,
     picked,
     table,
@@ -157,31 +155,34 @@
             )
 
         def one(step, carry):
-            half = step // classes
-            c = lax.rem(step, classes)
-            pis = [stat[c, i] for i in range(4)]
-
-            def factor(h, n):
-                return grow[c, offset[h] + 8 * n : offset[h] + 8 * n + 8, :]
+            half = step // (classes // 2)
+            pair = lax.rem(step, classes // 2) * 2
+            both = (0, 1)
+            pis = [[stat[pair + b, i] for i in range(4)] for b in both]
+
+            def factor(b, h, n):
+                return grow[pair + b, offset[h] + 8 * n : offset[h] + 8 * n + 8, :]
 
             def tip(n):
                 code = picked[half, 8 * n : 8 * n + 8, :]
                 marks = [code == float(i) for i in range(4)]
-                own = jnp.where(
-                    marks[0], pis[0], jnp.where(marks[1], pis[1], jnp.where(marks[2], pis[2], pis[3]))
-                )
-                off = factor(0, n) * own
-                on = off + 1.0
-                return [jnp.where(mark, on, off) for mark in marks]
-
-            def spread(values, scale):
-                mean = (values[0] * pis[0] + values[1] * pis[1]) + (
-                    values[2] * pis[2] + values[3] * pis[3]
+                result = []
+                for b in both:
+                    own = jnp.where(marks[2], pis[b][2], pis[b][3])
+                    own = jnp.where(marks[0], pis[b][0], jnp.where(marks[1], pis[b][1], own))
+                    off = factor(b, 0, n) * own
+                    on = off + 1.0
+                    result.append([jnp.where(mark, on, off) for mark in marks])
+                return result
+
+            def spread(b, values, scale):
+                mean = (values[0] * pis[b][0] + values[1] * pis[b][1]) + (
+                    values[2] * pis[b][2] + values[3] * pis[b][3]
                 )
                 move = scale * mean
                 return [value + move for value in values]
 
-            logs = []
+            logs = ([], [])
 
             def node(h, n):
                 if h == 0:
@@ -189,32 +190,39 @@
                 gap = (local >> h) // 8
                 left = node(h - 1, n)
                 right = node(h - 1, n + gap)
-                if h > 1:
-                    left = spread(left, factor(h - 1, n))
-                    right = spread(right, factor(h - 1, n + gap))
-                values = [a * b for a, b in zip(left, right)]
-                if h == 3:
-                    largest = jnp.maximum(
-                        jnp.maximum(values[0], values[1]), jnp.maximum(values[2], values[3])
-                    )
-                    scale = pl.reciprocal(largest, approx=True)
-                    logs.append(jnp.log(scale))
-                    values = [value * scale for value in values]
-                return values
-
-            values = spread(node(low - 1, 0), factor(low - 1, 0))
-            values = [value[0:clades] * value[clades : 2 * clades] for value in values]
-            log_sum = jnp.sum(sum(logs[1:], logs[0]), axis=0, keepdims=True)
-            log_sum = jnp.sum(jnp.log(values[3]), axis=0, keepdims=True) - log_sum
-            inverse = 1.0 / values[3]
-            for i in range(3):
-                ratio = values[i] * inverse
-                for j in range(clades):
-                    dest[j * 3 + i, pl.ds(step, 1), :] = ratio[j : j + 1]
-            dest[clades * 3, pl.ds(step, 1), :] = log_sum
+                result = []
+                for b in both:
+                    one_left, one_right = left[b], right[b]
+                    if h > 1:
+                        one_left = spread(b, one_left, factor(b, h - 1, n))
+                        one_right = spread(b, one_right, factor(b, h - 1, n + gap))
+                    values = [x * y for x, y in zip(one_left, one_right)]
+                    if h == 3:
+                        largest = jnp.maximum(
+                            jnp.maximum(values[0], values[1]), jnp.maximum(values[2], values[3])
+                        )
+                        scale = pl.reciprocal(largest, approx=True)
+                        logs[b].append(jnp.log(scale))
+                        values = [value * scale for value in values]
+                    result.append(values)
+                return result
+
+            ends = node(low - 1, 0)
+            for b in both:
+                row = pl.ds(half * classes + pair + b, 1)
+                values = spread(b, ends[b], factor(b, low - 1, 0))
+                values = [value[0:clades] * value[clades : 2 * clades] for value in values]
+                log_sum = jnp.sum(sum(logs[b][1:], logs[b][0]), axis=0, keepdims=True)
+                log_sum = jnp.sum(jnp.log(values[3]), axis=0, keepdims=True) - log_sum
+                inverse = 1.0 / values[3]
+                for i in range(3):
+                    ratio = values[i] * inverse
+                    for j in range(clades):
+                        dest[j * 3 + i, row, :] = ratio[j : j + 1]
+                dest[clades * 3, row, :] = log_sum
             return carry
 
-        lax.fori_loop(0, rows, one, 0)
+        lax.fori_loop(0, rows // 2, one, 0)
 
     copies = []
     for place, k in enumerate([2, 1, 3] if groups == 4 else range(1, groups)):
@@ -291,7 +299,7 @@
         top = jnp.max(a, axis=0, keepdims=True)
         total = top + jnp.log(jnp.sum(jnp.exp(a - top), axis=0, keepdims=True))
         n = counts_ref[pl.ds(g * halves + half, 1), :].astype(f32)
-        site_out[0:1, half * LANES : (half + 1) * LANES] = total / taxa
+        result[half : half + 1, :] = total / taxa
         mass = mass + n * jnp.exp(a - total)
         loglik = loglik + n * total
         seen = seen + n
@@ -342,8 +350,17 @@
     mean = line[classes : classes + 1] / (all_count * taxa)
     share = line[0:classes] / all_count
     mine = lax.broadcasted_iota(jnp.int32, (classes, 1), 0) == g
-    weight_out[0] = jnp.sum(jnp.where(mine, share, 0.0))
-    mean_out[0] = jnp.sum(mean)
+    share = jnp.sum(jnp.where(mine, share, 0.0), axis=0, keepdims=True)
+    result[halves : halves + 1, :] = jnp.broadcast_to(share, (1, LANES))
+    result[halves + 1 : halves + 2, :] = jnp.broadcast_to(mean, (1, LANES))
+
+
+def finish(result, site_out, weight_out, mean_out):
+    halves = result.shape[0] - 2
+    for half in range(halves):
+        site_out[0:1, half * LANES : (half + 1) * LANES] = result[half : half + 1, :]
+    weight_out[...] = result[halves : halves + 1, 0:1]
+    mean_out[...] = result[halves + 1 : halves + 2, 0:1]
 
 
 def solution(mesh):
@@ -366,15 +383,11 @@
         vmem = pl.BlockSpec(memory_space=pltpu.VMEM)
         smem = pl.BlockSpec(memory_space=pltpu.SMEM)
         f32 = jnp.float32
-        site_loglik, new_weights, mean_loglik = pl.pallas_call(
+        result = pl.pallas_call(
             functools.partial(kernel, groups, site_devices),
-            out_shape=(
-                jax.ShapeDtypeStruct((1, quarter), f32),
-                jax.ShapeDtypeStruct((1,), f32),
-                jax.ShapeDtypeStruct((1,), f32),
-            ),
+            out_shape=jax.ShapeDtypeStruct((halves + 2, LANES), f32),
             in_specs=[pl.BlockSpec(memory_space=pl.ANY), vmem, vmem, smem, vmem, vmem, vmem],
-            out_specs=(vmem, smem, smem),
+            out_specs=vmem,
             scratch_shapes=[
                 pltpu.VMEM((local, sites), jnp.int32),
                 pltpu.VMEM((halves, local, LANES), f32),
@@ -407,7 +420,17 @@
             frequencies,
             weights.reshape(1, classes),
         )
-        return site_loglik, new_weights, mean_loglik.reshape(())
+        site_loglik, new_weights, mean_loglik = pl.pallas_call(
+            finish,
+            out_shape=(
+                jax.ShapeDtypeStruct((1, quarter), f32),
+                jax.ShapeDtypeStruct((1, 1), f32),
+                jax.ShapeDtypeStruct((1, 1), f32),
+            ),
+            in_specs=[vmem],
+            out_specs=(vmem, vmem, vmem),
+        )(result)
+        return site_loglik, new_weights.reshape(1), mean_loglik.reshape(())
 
     return jax.shard_map(
         per_device,

time: 27.9 us -> 24.1 us (0.86)
  between operations: 4.14 us -> 0.64 us
  local copies, waits for them, and re-layouts: 1.21 us -> 0 us
  Pallas kernels: 22.3 us -> 23.3 us
    pallas_call x0 -> x1, Pallas kernels: none -> 1.24 us  [per_device(): pl.pallas_call(finish, out_shape=(jax.ShapeDtypeStruct((1, quarter), f32)...]
    unnamed x3 -> x0, local copies, waits for them, and re-layouts: 1.21 us -> none
where the time goes in v2:
time: 24.1 us; the launch traced here: 23.9 us
  Pallas kernels  23.3 us (97%)
  between operations  0.64 us (3%)
    pallas_call x1, Pallas kernels, per_device(): pl.pallas_call(functools.partial(kernel, groups, site_devices), out_shape...  22.1 us
    pallas_call x1, Pallas kernels, per_device(): pl.pallas_call(finish, out_shape=(jax.ShapeDtypeStruct((1, quarter), f32)...  1.24 us

profile of v2, /device:TPU:0, one launch (start us, length us, event | category | flops | bytes accessed | tf_op | source)
XLA Modules:
  0.0 23.9 jit_solution(7960195250028018550)
XLA Ops:
  0.6 22.1 %shard_map.85.result = f32[4,128]{1,0:T(4,128)} custom-call(s32[256,1024]{1,0:T(8,128)} %codes_hbm.1, s32[8,128]{1,0:T(8,128)} %bitcast.7, s32[2,1023]{1,0:T(2,128)} %bitcast.5, s32[2,1023]{1,0:T(2,128)} %bitcast.6, f32[4,2046]{1,0:T(4,128)} %lengths_ref.1, f32[4,4]{1,0:T(4,128)} %freq_ref.1, f32[1,4]{1,0:T(1,128)} %bitcast.8), custom_call_target="tpu_custom_call" | custom-call | tf_op jit(solution)/shard_map/pallas_call | solution.py:386
  22.7 1.2 %shard_map.86 = (f32[1,256]{1,0:T(1,128)}, f32[1,1]{1,0:T(1,128)}, f32[1,1]{1,0:T(1,128)}) custom-call(f32[4,128]{1,0:T(4,128)} %shard_map.85.result), custom_call_target="tpu_custom_call" | custom-call | tf_op jit(solution)/shard_map/pallas_call | solution.py:423
